TPU v7x, 512 devices: a whole 4x8x8 slice. The times are simulated.
512 devices in a mesh: ctx: 64 (over y, z_hi, core), head: 8 (over x, z_lo).
Axes of the slice: x: 4, y: 8, z: 8 (z_hi: 4, z_lo: 2; z = z_hi * 2 + z_lo), core: 2. Of those that a mesh axis runs over, the one named last changes fastest.
Arguments:
- queries: bfloat16 [1, 65536, 1024], P(None, ('ctx', 'head')), may hold values from -150 to 150
- keys: bfloat16 [1, 65536, 1024], P(None, ('ctx', 'head')), may hold values from -32 to 32
- values: bfloat16 [1, 65536, 1024], P(None, ('ctx', 'head')), may hold values from -6 to 6
- rates: float32 [1, 8, 65536], P(None, 'head', 'ctx'), may hold values from 0.0002 to 0.004
- tail_keys: bfloat16 [32768, 1024], P('ctx', 'head'), may hold values from -6 to 6
- tail_values: bfloat16 [32768, 1024], P('ctx', 'head'), may hold values from -6 to 6
- state_in_gu: float32 [64, 8, 2, 128, 256], P('ctx', 'head'), may hold values from -0.5 to 0.5
- state_in_down: float32 [64, 8, 256, 128], P('ctx', 'head'), may hold values from -0.375 to 0.375
- fresh_gu: float32 [8, 2, 128, 256], P('head'), may hold values from -0.5 to 0.5
- fresh_down: float32 [8, 256, 128], P('head'), may hold values from -0.375 to 0.375
- out_gain: float32 [1024], P('head'), may hold values from 0.1 to 1.9
- seq_ids: int32 [64, 2], replicated, may hold values from 0 to 127, as said below
- live_lengths: int32 [64, 1], replicated, may hold values from 1 to 1024, as said below
Outputs:
- mixed: bfloat16 [1, 65536, 1024], P(None, ('ctx', 'head'))
- state_out_gu: float32 [64, 8, 2, 128, 256], P('ctx', 'head')
- state_out_down: float32 [64, 8, 256, 128], P('ctx', 'head')
Inputs may be any that keep to these rules, and one draw needn't show every extreme that they name: `seq_ids`: block (c, t + 1) continues the sequence of block ((c - 1) mod 64, t) exactly when their numbers agree, else it begins a new sequence; different sequences have different numbers. `live_lengths`: only a block whose successor (device c + 1 mod 64, step t + 1) begins a new sequence is shorter than 1024; its live tokens are the first ones.
All inputs are finite; a program needn't handle non-finite values.
Results may differ from a plain program's by a relative error of at most 0.0028.
Values may be sent and summed in bfloat16 or wider, within the bound.
A program may use at most 64 MiB of HBM per device.

v0:
```python
import math

import jax
import jax.numpy as jnp
from jax import lax
from jax.sharding import PartitionSpec as P

epsilon = 1e-06


def from_behind(shard, axis, by):
    size = lax.axis_size(axis)
    return lax.ppermute(shard, axis, [(i, (i + by) % size) for i in range(size)])


def highest(left, right):
    return jnp.dot(left, right, precision=lax.Precision.HIGHEST)


def rms_rows(matrix):
    return matrix / jnp.sqrt(jnp.mean(matrix * matrix, axis=-1, keepdims=True) + epsilon)


def renormed(old_weight, new_weight):
    old_scale = jnp.sqrt(jnp.mean(old_weight * old_weight, axis=0, keepdims=True) + epsilon)
    new_scale = jnp.sqrt(jnp.mean(new_weight * new_weight, axis=0, keepdims=True) + epsilon)
    return new_weight * (old_scale / new_scale)


def fast_block(
    block_q,
    block_k,
    block_v,
    rate_row,
    prior_keys,
    prior_values,
    gate_up,
    down_proj,
    fresh_pair,
    fresh_proj,
    head_gain,
    length,
    linked,
):
    block_len = block_q.shape[0]
    window = prior_keys.shape[0]
    head_dim = block_q.shape[1]
    gate_up = jnp.where(linked, gate_up, fresh_pair)
    down_proj = jnp.where(linked, down_proj, fresh_proj)
    joined_keys = jnp.concatenate([prior_keys, block_k], axis=0)
    joined_values = jnp.concatenate([prior_values, block_v], axis=0)
    row_index = jnp.arange(window)[:, None]
    col_index = jnp.arange(2 * window)[None, :]
    pieces = []
    for offset in range(0, block_len, window):
        query_pos = offset + row_index
        key_pos = offset - window + col_index
        allowed = (
            (key_pos <= query_pos)
            & (key_pos > query_pos - window)
            & ((key_pos < length) | (key_pos == query_pos))
            & ((key_pos >= 0) | linked)
        )
        scores = jnp.einsum(
            "qd,kd->qk",
            block_q[offset : offset + window],
            joined_keys[offset : offset + 2 * window],
            preferred_element_type=jnp.float32,
        ) * (1.0 / math.sqrt(head_dim))
        scores = jnp.where(allowed, scores, -1e30)
        largest = jnp.max(scores, axis=-1, keepdims=True)
        exponent = jnp.exp(scores - largest)
        weights = (exponent / jnp.sum(exponent, axis=-1, keepdims=True)).astype(jnp.bfloat16)
        pieces.append(
            jnp.dot(
                weights,
                joined_values[offset : offset + 2 * window],
                preferred_element_type=jnp.float32,
            )
        )
    attended = jnp.concatenate(pieces, axis=0)
    query_unit = rms_rows(block_q.astype(jnp.float32))
    key_unit = rms_rows(block_k.astype(jnp.float32))
    w_gate = gate_up[0]
    w_up = gate_up[1]
    fast_out = highest(
        jax.nn.silu(highest(query_unit, w_gate)) * highest(query_unit, w_up), down_proj
    )
    live_rows = (jnp.arange(block_len) < length).astype(jnp.float32)[:, None]
    mixed = ((attended + rms_rows(fast_out) * head_gain) * live_rows).astype(jnp.bfloat16)
    key_gate = highest(key_unit, w_gate)
    key_up = highest(key_unit, w_up)
    gate_sigmoid = jax.nn.sigmoid(key_gate)
    gate_act = key_gate * gate_sigmoid
    out_grad = -(rate_row[:, None] * live_rows) * block_v.astype(jnp.float32)
    grad_down = highest((gate_act * key_up).T, out_grad)
    hidden_grad = highest(out_grad, down_proj.T)
    grad_up = highest(key_unit.T, hidden_grad * gate_act)
    grad_gate = highest(
        key_unit.T, hidden_grad * key_up * gate_sigmoid * (1.0 + key_gate * (1.0 - gate_sigmoid))
    )
    new_pair = jnp.stack([renormed(w_gate, w_gate - grad_gate), renormed(w_up, w_up - grad_up)])
    new_down = renormed(down_proj, down_proj - grad_down)
    return (mixed, new_pair, new_down)


def advance(
    block_q,
    block_k,
    block_v,
    rate_row,
    prior_keys,
    prior_values,
    gate_up,
    down_proj,
    fresh_pair,
    fresh_proj,
    head_gain,
    length,
    linked,
):
    moved_pair, moved_proj = from_behind((gate_up, down_proj), "ctx", 1)
    return fast_block(
        block_q,
        block_k,
        block_v,
        rate_row,
        prior_keys,
        prior_values,
        moved_pair,
        moved_proj,
        fresh_pair,
        fresh_proj,
        head_gain,
        length,
        linked,
    )


def on_device(
    queries,
    keys,
    values,
    rates,
    tail_keys,
    tail_values,
    state_in_gu,
    state_in_down,
    fresh_gu,
    fresh_down,
    out_gain,
    seq_ids,
    live_lengths,
):
    steps_total = queries.shape[0]
    ctx_count = lax.axis_size("ctx")
    here_index = lax.axis_index("ctx")
    before_index = (here_index + ctx_count - 1) % ctx_count
    own_ids = lax.dynamic_index_in_dim(seq_ids, here_index, 0, keepdims=False)
    prior_ids = lax.dynamic_index_in_dim(seq_ids, before_index, 0, keepdims=False)
    own_lengths = lax.dynamic_index_in_dim(live_lengths, here_index, 0, keepdims=False)
    window = tail_keys.shape[0]
    gate_up = state_in_gu[0, 0]
    down_proj = state_in_down[0, 0]
    fresh_pair = fresh_gu[0]
    fresh_proj = fresh_down[0]
    local_q, local_k, local_v = (
        lax.all_to_all(queries, "head", split_axis=2, concat_axis=1, tiled=True),
        lax.all_to_all(keys, "head", split_axis=2, concat_axis=1, tiled=True),
        lax.all_to_all(values, "head", split_axis=2, concat_axis=1, tiled=True),
    )
    block_len = local_q.shape[1]
    source_keys = jnp.concatenate(
        [tail_keys[None], local_k[: steps_total - 1, block_len - window :]], axis=0
    )
    source_values = jnp.concatenate(
        [tail_values[None], local_v[: steps_total - 1, block_len - window :]], axis=0
    )
    prior_key_all, prior_value_all = from_behind((source_keys, source_values), "ctx", 1)
    linked = own_ids[1] == prior_ids[0]
    mixed_step, gate_up, down_proj = advance(
        local_q[0],
        local_k[0],
        local_v[0],
        rates[0, 0],
        prior_key_all[0],
        prior_value_all[0],
        gate_up,
        down_proj,
        fresh_pair,
        fresh_proj,
        out_gain,
        own_lengths[0],
        linked,
    )
    results = [mixed_step]
    mixed = lax.all_to_all(jnp.stack(results), "head", split_axis=1, concat_axis=2, tiled=True)
    return (mixed, gate_up[None, None], down_proj[None, None])


def solution(mesh):
    placed = (
        P(None, ("ctx", "head"), None),
        P(None, ("ctx", "head"), None),
        P(None, ("ctx", "head"), None),
        P(None, "head", "ctx"),
        P("ctx", "head"),
        P("ctx", "head"),
        P("ctx", "head", None, None, None),
        P("ctx", "head", None, None),
        P("head", None, None, None),
        P("head", None, None),
        P("head"),
        P(),
        P(),
    )
    return jax.shard_map(
        on_device,
        mesh=mesh,
        in_specs=placed,
        out_specs=(
            P(None, ("ctx", "head"), None),
            P("ctx", "head", None, None, None),
            P("ctx", "head", None, None),
        ),
        check_vma=False,
    )
```

profile of v0, /device:TPU:48, one launch (start us, length us, event | category | flops | bytes accessed | tf_op | source)
XLA Modules:
  0.0 102.0 jit_solution(8273138698115083297)
XLA Ops:
  0.7 2.1 %collective-permute-start.2 = (f32[2,128,256]{2,1,0:T(8,128)}, f32[2,128,256]{2,1,0:T(8,128)S(1)}, u32[]{:S(2)}, u32[]{:S(2)}) collective-permute-start(f32[2,128,256]{2,1,0:T(8,128)} %bitcast.117), channel_id=1, source_target_pairs={{0,8},{8,16},{16,24},{24,32},{32,40},{40,48},{48,56},{56,64},{64,7... | collective-permute-start | bytes 786440 | tf_op jit(solution)/shard_map/ppermute | solution.py:13
  2.7 1.3 %copy.59 = bf16[1,128,1024]{1,0,2:T(2,128)(2,1)S(1)} copy(bf16[1,128,1024]{2,1,0:T(8,128)(2,1)} %param.14) | data formatting | bytes 524288 | tf_op args[1]
  4.0 0.5 broadcast.266
  4.5 2.2 %reduce.4 = bf16[1024,128]{1,0:T(8,128)(2,1)S(1)} reduce(bf16[1024,1,128]{2,1,0:T(2,128)(2,1)S(1)} %bitcast.99, bf16[]{:T(256)} %broadcast.266), dimensions={1}, to_apply=%bitcast.68.reduce_sub_computation | reduce | bytes 524290
  6.7 0.8 reshape.196
  7.5 6.1 %all-to-all-start = ((bf16[8,2,8192]{2,1,0:T(2,128)(2,1)}), bf16[8,2,8192]{2,1,0:T(2,128)(2,1)S(1)}, u32[]{:S(2)}, u32[]{:S(2)}) async-start(bf16[8,2,8192]{2,1,0:T(2,128)(2,1)} %reshape.196), calls=%async_computation | async-start | bytes 524288 | tf_op jit(solution)/shard_map/all_to_all | solution.py:169
  13.6 5.9 %collective-permute-start.3 = (f32[256,128]{1,0:T(8,128)S(1)}, f32[256,128]{1,0:T(8,128)S(1)}, u32[]{:S(2)}, u32[]{:S(2)}) collective-permute-start(f32[256,128]{1,0:T(8,128)S(1)} %bitcast.118), channel_id=1, source_target_pairs={{0,8},{8,16},{16,24},{24,32},{32,40},{40,48},{48,56},{56,64},{64,7... | collective-permute-start | bytes 393224 | tf_op jit(solution)/shard_map/ppermute | solution.py:13
  19.5 2.2 %collective-permute-start = (bf16[1,512,128]{2,1,0:T(8,128)(2,1)}, bf16[1,512,128]{2,1,0:T(8,128)(2,1)}, u32[]{:S(2)}, u32[]{:S(2)}) collective-permute-start(bf16[1,512,128]{2,1,0:T(8,128)(2,1)} %bitcast.2), channel_id=1, source_target_pairs={{0,8},{8,16},{16,24},{24,32},{32,40},{40,48},{48,56},{56,64},{64,7... | collective-permute-start | bytes 393224 | tf_op jit(solution)/shard_map/ppermute | solution.py:13
  21.7 6.2 %collective-permute-start.1 = (bf16[1,512,128]{2,1,0:T(8,128)(2,1)}, bf16[1,512,128]{2,1,0:T(8,128)(2,1)}, u32[]{:S(2)}, u32[]{:S(2)}) collective-permute-start(bf16[1,512,128]{2,1,0:T(8,128)(2,1)} %bitcast.9), channel_id=1, source_target_pairs={{0,8},{8,16},{16,24},{24,32},{32,40},{40,48},{48,56},{56,64},{64,7... | collective-permute-start | bytes 393224 | tf_op jit(solution)/shard_map/ppermute | solution.py:13
  28.0 0.6 iota_add_fusion
  28.6 0.6 iota_add_fusion.2
  29.2 0.6 iota_add_fusion.1
  29.8 0.5 slice.32
  30.4 0.5 slice.33
  30.9 0.6 constant_dynamic-slice_fusion.2
  31.5 0.6 fusion.48
  32.1 0.7 select_negate_fusion
  34.1 1.2 %compare_or_fusion = (pred[1024]{0:T(1024)(128)(4,1)}, pred[1024]{0:T(1024)(128)(4,1)}) fusion(pred[]{:T(512)} %bitcast.1, s32[]{:T(128)} %bitcast), kind=kLoop, calls=%fused_computation.90 | loop fusion | flops 4096 | bytes 2053 | tf_op jit(solution)/shard_map/or | solution.py:62
  35.3 1.2 %iota_compare_fusion.5 = pred[1024]{0:T(1024)(128)(4,1)} fusion(s32[]{:T(128)} %bitcast), kind=kLoop, calls=%fused_computation.88 | loop fusion | flops 1024 | bytes 1028 | tf_op jit(solution)/shard_map/lt | solution.py:61
  37.0 2.2 %reduce.3 = bf16[1024,128]{1,0:T(8,128)(2,1)S(1)} reduce(bf16[1024,1,128]{2,1,0:T(2,128)(2,1)S(1)} %bitcast.101, bf16[]{:T(256)} %broadcast.266), dimensions={1}, to_apply=%bitcast.66.reduce_sub_computation | reduce | bytes 524290
  39.2 0.8 reshape.194
  40.4 2.2 %reduce.2 = bf16[1024,128]{1,0:T(8,128)(2,1)S(1)} reduce(bf16[1024,1,128]{2,1,0:T(2,128)(2,1)S(1)} %bitcast.102, bf16[]{:T(256)} %broadcast.266), dimensions={1}, to_apply=%bitcast.64.reduce_sub_computation | reduce | bytes 524290
  42.6 0.8 reshape.192
  43.3 0.6 multiply_reduce_fusion.2
  44.0 5.4 %all-to-all-start.2 = ((bf16[8,2,8192]{2,1,0:T(2,128)(2,1)}), bf16[8,2,8192]{2,1,0:T(2,128)(2,1)S(1)}, u32[]{:S(2)}, u32[]{:S(2)}) async-start(bf16[8,2,8192]{2,1,0:T(2,128)(2,1)} %reshape.194), calls=%async_computation.2 | async-start | bytes 524288 | tf_op jit(solution)/shard_map/all_to_all | solution.py:170
  50.3 1.0 fusion.43
  51.3 2.0 %fusion.45 = f32[1024,256]{1,0:T(8,128)} fusion(f32[1024,128]{1,0:T(8,128)S(1)} %bitcast.92, f32[2,128,256]{2,1,0:T(8,128)S(1)} %bitcast_select_fusion.1), kind=kOutput, calls=%fused_computation.82 | convolution fusion | flops 402653184 | bytes 1703936 | tf_op jit(solution)/shard_map/dot_general | solution.py:17
  53.2 4.2 %all-to-all-done.2 = bf16[8,2,8192]{2,1,0:T(2,128)(2,1)S(1)} async-done(((bf16[8,2,8192]{2,1,0:T(2,128)(2,1)}), bf16[8,2,8192]{2,1,0:T(2,128)(2,1)S(1)}, u32[]{:S(2)}, u32[]{:S(2)}) %all-to-all-start.2) | async-done | bytes 262176 | tf_op jit(solution)/shard_map/all_to_all | solution.py:170
  57.4 3.6 %all-to-all-start.1 = ((bf16[8,2,8192]{2,1,0:T(2,128)(2,1)}), bf16[8,2,8192]{2,1,0:T(2,128)(2,1)S(1)}, u32[]{:S(2)}, u32[]{:S(2)}) async-start(bf16[8,2,8192]{2,1,0:T(2,128)(2,1)} %reshape.192), calls=%async_computation.1 | async-start | bytes 524288 | tf_op jit(solution)/shard_map/all_to_all | solution.py:168
  61.6 1.0 %fusion.31 = f32[1024,256]{1,0:T(8,128)S(1)} fusion(f32[256,128]{1,0:T(8,128)S(1)} %get-tuple-element.9, bf16[1024,128]{1,0:T(8,128)(2,1)S(1)} %bitcast.106, f32[1024]{0:T(1024)S(1)} %select_negate_fusion), kind=kOutput, calls=%fused_computation.52 | convolution fusion | flops 402915328 | bytes 1445888 | tf_op jit(solution)/shard_map/dot_general | solution.py:17
  62.6 2.5 %multiply_reduce_fusion.3 = (f32[256]{0:T(256)}, f32[128,256]{1,0:T(8,128)}) fusion(f32[1024,256]{1,0:T(8,128)S(1)} %fusion.31, f32[1024,256]{1,0:T(8,128)S(1)} %fusion.43, bf16[1024,128]{1,0:T(8,128)(2,1)S(1)} %bitcast.110, f32[1024]{0:T(1024)S(1)} %get-tuple-element.13, f32[2,128,256]{2,1,0:T(8,128)S(1)} %bitcast_select_fusion.1), kind=kOutput, calls=%fused_computation.75 | convolution fusion | flops 404324096 | bytes 2626560 | tf_op jit(solution)/shard_map/dot_general | solution.py:17
  65.2 3.3 %multiply_reduce_fusion.1 = (f32[128]{0:T(128)}, f32[256,128]{1,0:T(8,128)}) fusion(f32[256,128]{1,0:T(8,128)S(1)} %get-tuple-element.9, bf16[1024,128]{1,0:T(8,128)(2,1)S(1)} %bitcast.107, f32[1024]{0:T(1024)S(1)} %select_negate_fusion, f32[1024,256]{1,0:T(8,128)S(1)} %copy-done.1, f32[1024,256]{1,0:T(8,128)S(1)} %fusion.43), kind=kOutput, calls=%fused_computation.72 | convolution fusion | flops 404324224 | bytes 2626048 | tf_op jit(solution)/shard_map/dot_general | solution.py:17
  68.4 2.7 %multiply_reduce_fusion.5 = (f32[256]{0:T(256)}, f32[128,256]{1,0:T(8,128)}) fusion(f32[1024,256]{1,0:T(8,128)S(1)} %fusion.43, f32[1024,256]{1,0:T(8,128)S(1)} %fusion.31, f32[1024,256]{1,0:T(8,128)S(1)} %copy-done.1, bf16[1024,128]{1,0:T(8,128)(2,1)S(1)} %bitcast.111, f32[1024]{0:T(1024)S(1)} %get-tuple-element.13, ...), kind=kOutput, calls=%fused_computation.78 | convolution fusion | flops 405372672 | bytes 3675136 | tf_op jit(solution)/shard_map/dot_general | solution.py:17
  72.0 1.0 fusion.44
  73.0 1.0 fusion.46
  74.0 0.8 copy.62
  74.8 2.1 %multiply_reduce_fusion = (f32[1024]{0:T(1024)}, f32[1024,128]{0,1:T(8,128)S(1)}) fusion(f32[256,128]{1,0:T(8,128)S(1)} %get-tuple-element.9, f32[1024,256]{1,0:T(8,128)S(1)} %fusion.46, f32[1024,256]{1,0:T(8,128)S(1)} %fusion.44), kind=kOutput, calls=%fused_computation.54 | convolution fusion | flops 404225024 | bytes 2756608 | tf_op jit(solution)/shard_map/dot_general | solution.py:17
  77.2 1.8 %fusion.57 = (f32[512]{0:T(512)S(1)}, f32[512,1024]{0,1:T(8,128)S(1)}) fusion(bf16[512,128]{1,0:T(8,128)(2,1)S(1)} %bitcast.115, bf16[1024,128]{1,0:T(8,128)(2,1)} %bitcast.112, pred[1024]{0:T(1024)(128)(4,1)} %iota_compare_fusion.5, s32[512]{0:T(512)} %iota_add_fusion.1), kind=kOutput, calls=%fused_computation.109 | convolution fusion | flops 138935808 | bytes 2495488 | tf_op jit(solution)/shard_map/qd,kd->qk/dot_general | solution.py:64
  79.4 0.5 fusion.26
  80.3 2.0 %fusion.58 = (f32[512]{0:T(512)S(1)}, f32[512,1024]{0,1:T(8,128)S(1)}) fusion(bf16[512,128]{1,0:T(8,128)(2,1)S(1)} %bitcast.114, bf16[1024,128]{1,0:T(8,128)(2,1)S(1)} %bitcast.113, bf16[512,128]{1,0:T(8,128)(2,1)} %bitcast.3, pred[1024]{0:T(1024)(128)(4,1)S(1)} %copy-done.17, pred[1024]{0:T(1024)(128)(4,1)S(1)} %copy-done.18, s32[512]{0:T(512)S(1)} %copy-done.16, ...), kind=kOutput, calls=%fused_computation.110 | convolution fusion | flops 139984384 | bytes 2631680 | tf_op jit(solution)/shard_map/qd,kd->qk/dot_general | solution.py:64
  82.7 1.4 %fusion.25 = f32[512,128]{1,0:T(8,128)S(1)} fusion(f32[512,1024]{0,1:T(8,128)S(1)} %get-tuple-element.21, f32[512]{0:T(512)S(1)} %fusion.7, f32[512]{0:T(512)S(1)} %get-tuple-element.20, bf16[1024,128]{1,0:T(8,128)(2,1)S(1)} %bitcast.109, bf16[512,128]{1,0:T(8,128)(2,1)} %bitcast.10), kind=kOutput, calls=%fused_computation.40 | convolution fusion | flops 136314880 | bytes 2756608 | tf_op jit(solution)/shard_map/dot_general | solution.py:75
  85.0 2.2 %reduce.5 = bf16[1024,128]{1,0:T(8,128)(2,1)S(1)} reduce(bf16[1024,1,128]{2,1,0:T(2,128)(2,1)S(1)} %bitcast.100, bf16[]{:T(256)} %broadcast.266), dimensions={1}, to_apply=%bitcast.84.reduce_sub_computation | reduce | bytes 524290
  87.2 0.8 reshape.198
  87.9 5.4 %all-to-all-start.3 = ((bf16[8,2,8192]{2,1,0:T(2,128)(2,1)}), bf16[8,2,8192]{2,1,0:T(2,128)(2,1)S(1)}, u32[]{:S(2)}, u32[]{:S(2)}) async-start(bf16[8,2,8192]{2,1,0:T(2,128)(2,1)} %reshape.198), calls=%async_computation.3 | async-start | bytes 524288 | tf_op jit(solution)/shard_map/all_to_all | solution.py:197
  93.5 0.7 maximum_bitcast_fusion
  94.2 0.7 multiply_bitcast_fusion
  94.9 5.8 %all-to-all-done.3 = bf16[8,2,8192]{2,1,0:T(2,128)(2,1)S(1)} async-done(((bf16[8,2,8192]{2,1,0:T(2,128)(2,1)}), bf16[8,2,8192]{2,1,0:T(2,128)(2,1)S(1)}, u32[]{:S(2)}, u32[]{:S(2)}) %all-to-all-start.3) | async-done | bytes 262176 | tf_op jit(solution)/shard_map/all_to_all | solution.py:197
  101.2 0.9 copy.72
  (92 shorter events, 5.9 us)
Async XLA Ops:
  0.6 30.2 %copy-start = (s32[64,1]{0,1:T(1,128)S(1)}, s32[64,1]{0,1:T(1,128)}, u32[]{:S(2)}) copy-start(s32[64,1]{0,1:T(1,128)} %param.25) | copy-start | bytes 772
  0.6 13.0 %copy-start.23 = (f32[1,1,256,128]{3,2,1,0:T(8,128)S(1)}, f32[1,1,256,128]{3,2,1,0:T(8,128)}, u32[]{:S(2)}) copy-start(f32[1,1,256,128]{3,2,1,0:T(8,128)} %param.20) | copy-start | bytes 393220
  0.7 29.1 %copy-start.15 = (s32[64,2]{0,1:T(2,128)S(1)}, s32[64,2]{0,1:T(2,128)}, u32[]{:S(2)}) copy-start(s32[64,2]{0,1:T(2,128)} %param.24) | copy-start | bytes 1540
  0.7 31.4 %copy-start.12 = (f32[1,1,1024]{2,1,0:T(1,128)S(1)}, f32[1,1,1024]{2,1,0:T(1,128)}, u32[]{:S(2)}) copy-start(f32[1,1,1024]{2,1,0:T(1,128)} %param.16) | copy-start | bytes 12292
  0.7 35.9 %copy-start.2 = (bf16[1,128,1024]{2,1,0:T(8,128)(2,1)S(1)}, bf16[1,128,1024]{2,1,0:T(8,128)(2,1)}, u32[]{:S(2)}) copy-start(bf16[1,128,1024]{2,1,0:T(8,128)(2,1)} %param.15) | copy-start | bytes 786436
  0.7 43.2 %collective-permute-start.2 = (f32[2,128,256]{2,1,0:T(8,128)}, f32[2,128,256]{2,1,0:T(8,128)S(1)}, u32[]{:S(2)}, u32[]{:S(2)}) collective-permute-start(f32[2,128,256]{2,1,0:T(8,128)} %bitcast.117), channel_id=1, source_target_pairs={{0,8},{8,16},{16,24},{24,32},{32,40},{40,48},{48,56},{56,64},{64,7... | collective-permute-start | bytes 786440 | tf_op jit(solution)/shard_map/ppermute | solution.py:13
  4.0 36.0 %copy-start.3 = (bf16[1,128,1024]{2,1,0:T(8,128)(2,1)S(1)}, bf16[1,128,1024]{2,1,0:T(8,128)(2,1)}, u32[]{:S(2)}) copy-start(bf16[1,128,1024]{2,1,0:T(8,128)(2,1)} %param.13) | copy-start | bytes 786436
  7.5 36.5 %all-to-all-start = ((bf16[8,2,8192]{2,1,0:T(2,128)(2,1)}), bf16[8,2,8192]{2,1,0:T(2,128)(2,1)S(1)}, u32[]{:S(2)}, u32[]{:S(2)}) async-start(bf16[8,2,8192]{2,1,0:T(2,128)(2,1)} %reshape.196), calls=%async_computation | async-start | bytes 524288 | tf_op jit(solution)/shard_map/all_to_all | solution.py:169
  13.6 29.7 %collective-permute-start.3 = (f32[256,128]{1,0:T(8,128)S(1)}, f32[256,128]{1,0:T(8,128)S(1)}, u32[]{:S(2)}, u32[]{:S(2)}) collective-permute-start(f32[256,128]{1,0:T(8,128)S(1)} %bitcast.118), channel_id=1, source_target_pairs={{0,8},{8,16},{16,24},{24,32},{32,40},{40,48},{48,56},{56,64},{64,7... | collective-permute-start | bytes 393224 | tf_op jit(solution)/shard_map/ppermute | solution.py:13
  19.5 60.5 %collective-permute-start = (bf16[1,512,128]{2,1,0:T(8,128)(2,1)}, bf16[1,512,128]{2,1,0:T(8,128)(2,1)}, u32[]{:S(2)}, u32[]{:S(2)}) collective-permute-start(bf16[1,512,128]{2,1,0:T(8,128)(2,1)} %bitcast.2), channel_id=1, source_target_pairs={{0,8},{8,16},{16,24},{24,32},{32,40},{40,48},{48,56},{56,64},{64,7... | collective-permute-start | bytes 393224 | tf_op jit(solution)/shard_map/ppermute | solution.py:13
  21.7 61.0 %collective-permute-start.1 = (bf16[1,512,128]{2,1,0:T(8,128)(2,1)}, bf16[1,512,128]{2,1,0:T(8,128)(2,1)}, u32[]{:S(2)}, u32[]{:S(2)}) collective-permute-start(bf16[1,512,128]{2,1,0:T(8,128)(2,1)} %bitcast.9), channel_id=1, source_target_pairs={{0,8},{8,16},{16,24},{24,32},{32,40},{40,48},{48,56},{56,64},{64,7... | collective-permute-start | bytes 393224 | tf_op jit(solution)/shard_map/ppermute | solution.py:13
  36.6 6.8 %copy-start.7 = (f32[1,256,128]{2,1,0:T(8,128)S(1)}, f32[1,256,128]{2,1,0:T(8,128)}, u32[]{:S(2)}) copy-start(f32[1,256,128]{2,1,0:T(8,128)} %param.22) | copy-start | bytes 393220
  37.0 7.0 %copy-start.6 = (f32[1,2,128,256]{3,2,1,0:T(8,128)S(1)}, f32[1,2,128,256]{3,2,1,0:T(8,128)}, u32[]{:S(2)}) copy-start(f32[1,2,128,256]{3,2,1,0:T(8,128)} %param.21) | copy-start | bytes 786436
  44.0 13.4 %all-to-all-start.2 = ((bf16[8,2,8192]{2,1,0:T(2,128)(2,1)}), bf16[8,2,8192]{2,1,0:T(2,128)(2,1)S(1)}, u32[]{:S(2)}, u32[]{:S(2)}) async-start(bf16[8,2,8192]{2,1,0:T(2,128)(2,1)} %reshape.194), calls=%async_computation.2 | async-start | bytes 524288 | tf_op jit(solution)/shard_map/all_to_all | solution.py:170
  50.0 18.4 %copy-start.4 = (bf16[1,8,128,128]{3,2,1,0:T(8,128)(2,1)}, bf16[1,8,128,128]{3,2,1,0:T(8,128)(2,1)S(1)}, u32[]{:S(2)}) copy-start(bf16[1,8,128,128]{3,2,1,0:T(8,128)(2,1)S(1)} %copy.60) | copy-start | bytes 786436
  57.4 13.7 %all-to-all-start.1 = ((bf16[8,2,8192]{2,1,0:T(2,128)(2,1)}), bf16[8,2,8192]{2,1,0:T(2,128)(2,1)S(1)}, u32[]{:S(2)}, u32[]{:S(2)}) async-start(bf16[8,2,8192]{2,1,0:T(2,128)(2,1)} %reshape.192), calls=%async_computation.1 | async-start | bytes 524288 | tf_op jit(solution)/shard_map/all_to_all | solution.py:168
  62.6 2.6 %copy-start.1 = (f32[1024,256]{1,0:T(8,128)S(1)}, f32[1024,256]{1,0:T(8,128)}, u32[]{:S(2)}) copy-start(f32[1024,256]{1,0:T(8,128)} %fusion.45) | copy-start | bytes 3145732
  79.3 0.7 copy-start.14
  79.3 1.0 copy-start.5
  79.3 1.0 copy-start.11
  79.3 1.0 copy-start.13
  79.3 1.0 copy-start.16
  79.4 1.0 copy-start.17
  79.4 1.0 copy-start.18
  82.7 1.4 %copy-start.21 = (f32[128]{0:T(128)S(1)}, f32[128]{0:T(128)}, u32[]{:S(2)}) copy-start(f32[128]{0:T(128)} %param.23) | copy-start | bytes 1540
  84.2 9.2 %copy-start.19 = (f32[256]{0:T(256)S(1)}, f32[256]{0:T(256)}, u32[]{:S(2)}) copy-start(f32[256]{0:T(256)} %get-tuple-element.22) | copy-start | bytes 3076
  84.2 9.2 %copy-start.20 = (f32[256]{0:T(256)S(1)}, f32[256]{0:T(256)}, u32[]{:S(2)}) copy-start(f32[256]{0:T(256)} %get-tuple-element.24) | copy-start | bytes 3076
  84.2 9.2 %copy-start.10 = (f32[128,256]{1,0:T(8,128)S(1)}, f32[128,256]{1,0:T(8,128)}, u32[]{:S(2)}) copy-start(f32[128,256]{1,0:T(8,128)} %get-tuple-element.25) | copy-start | bytes 393220
  84.2 9.3 %copy-start.9 = (f32[128,256]{1,0:T(8,128)S(1)}, f32[128,256]{1,0:T(8,128)}, u32[]{:S(2)}) copy-start(f32[128,256]{1,0:T(8,128)} %get-tuple-element.23) | copy-start | bytes 393220
  84.5 9.7 %copy-start.22 = (f32[128]{0:T(128)S(1)}, f32[128]{0:T(128)}, u32[]{:S(2)}) copy-start(f32[128]{0:T(128)} %get-tuple-element.8) | copy-start | bytes 1540
  84.5 9.7 %copy-start.24 = (f32[128]{0:T(128)S(1)}, f32[128]{0:T(128)}, u32[]{:S(2)}) copy-start(f32[128]{0:T(128)} %get-tuple-element.26) | copy-start | bytes 1540
  84.6 9.7 %copy-start.8 = (f32[256,128]{1,0:T(8,128)S(1)}, f32[256,128]{1,0:T(8,128)}, u32[]{:S(2)}) copy-start(f32[256,128]{1,0:T(8,128)} %get-tuple-element.27) | copy-start | bytes 393220
  87.9 12.7 %all-to-all-start.3 = ((bf16[8,2,8192]{2,1,0:T(2,128)(2,1)}), bf16[8,2,8192]{2,1,0:T(2,128)(2,1)S(1)}, u32[]{:S(2)}, u32[]{:S(2)}) async-start(bf16[8,2,8192]{2,1,0:T(2,128)(2,1)} %reshape.198), calls=%async_computation.3 | async-start | bytes 524288 | tf_op jit(solution)/shard_map/all_to_all | solution.py:197
where the time goes:
time: 103 us; the launch traced here: 102 us
  starting transfers between devices  36.9 us (36%)
  matrix products  22.2 us (22%)
  other arithmetic  17.7 us (17%)
  local copies, waits for them, and re-layouts  12.6 us (12%)
  waiting for transfers between devices  10 us (10%)
  between operations  2.57 us (2%)
    dot_general x9, matrix products, highest(): return jnp.dot(left, right, precision=lax.Precision.HIGHEST)  16.5 us
    ppermute x4, starting transfers between devices, from_behind(): lax.ppermute(shard, axis, [(i, (i + by) % size) for i in range(size)])  16.4 us
    unnamed x4, other arithmetic  8.81 us
    unnamed x67, local copies, waits for them, and re-layouts  8.44 us
    all_to_all x1, starting transfers between devices, on_device(): lax.all_to_all(keys, 'head', split_axis=2, concat_axis=1, tiled=True)  6.11 us
    all_to_all x1, waiting for transfers between devices, on_device(): lax.all_to_all(jnp.stack(results), 'head', split_axis=1, concat_axis=2, t...  5.77 us
    all_to_all x1, starting transfers between devices, on_device(): lax.all_to_all(jnp.stack(results), 'head', split_axis=1, concat_axis=2, t...  5.43 us
    all_to_all x1, starting transfers between devices, on_device(): lax.all_to_all(values, 'head', split_axis=2, concat_axis=1, tiled=True)  5.42 us
  transfers between devices with their start and end apart: 8, of which 2 were waited for; matrix products, arithmetic and copies ran while one was open for 45% of the time, Pallas kernels for 0%

commit v1 on v0

v1 whole, which is shorter than its diff:
```python
import math

import jax
import jax.numpy as jnp
from jax import lax
from jax.experimental import pallas as pl
from jax.experimental.pallas import tpu as pltpu
from jax.sharding import PartitionSpec as P

MESH = pl.DeviceIdType.MESH
EPS = 1e-06
NEG = -1e30
HD = 128
HID = 256
BLOCK = 1024
WIN = 512
TILE = 256
X_SIZE = 4
Z_SIZE = 2
PEERS = tuple((dx, dz) for dz in (1, 0) for dx in (2, 1, 3, 0) if (dx, dz) != (0, 0))


def nt(left, right):
    return lax.dot_general(left, right, (((1,), (1,)), ((), ())), preferred_element_type=jnp.float32)


def nn(left, right):
    return jnp.dot(left, right, preferred_element_type=jnp.float32)


def split(matrix):
    high = matrix.astype(jnp.bfloat16)
    low = (matrix - high.astype(jnp.float32)).astype(jnp.bfloat16)
    return high, low


def sigmoid(x):
    return 0.5 * jnp.tanh(0.5 * x) + 0.5


def kernel(
    ctx_count,
    q_ref, k_ref, v_ref, rate_ref, tail_k_ref, tail_v_ref, gu_ref, down_ref,
    fresh_gu_ref, fresh_down_ref, gain_ref, seq_ref, len_ref,
    mixed_ref, gu_out_ref, down_out_ref,
    q_buf, k_buf, v_buf, gu_buf, down_buf, fgu_buf, fdown_buf, out_buf, part_buf,
    local_sem, send_sem, recv_sem, out_send_sem, out_recv_sem,
):
    c = lax.axis_index("ctx")
    h = lax.axis_index("head")
    succ = lax.rem(c + 1, ctx_count)
    pred = lax.rem(c + ctx_count - 1, ctx_count)
    hx, hz = h // Z_SIZE, lax.rem(h, Z_SIZE)
    to_peer = [
        lax.rem(hx + dx, X_SIZE) * Z_SIZE + lax.rem(hz + dz, Z_SIZE) for dx, dz in PEERS
    ]
    from_peer = [
        lax.rem(hx + X_SIZE - dx, X_SIZE) * Z_SIZE + lax.rem(hz + dz, Z_SIZE) for dx, dz in PEERS
    ]
    n_peer = len(PEERS)

    barrier = pltpu.get_barrier_semaphore()
    for peer in to_peer:
        pl.semaphore_signal(barrier, inc=1, device_id=(c, peer), device_id_type=MESH)
    for other in (succ, pred):
        pl.semaphore_signal(barrier, inc=1, device_id=(other, h), device_id_type=MESH)

    def block(index):
        return pl.ds(pl.multiple_of(index * HD, HD), HD)

    def rows(index, base):
        return pl.ds(pl.multiple_of(base + index * HD, HD), HD)

    streams = ((k_ref, k_buf, WIN), (v_ref, v_buf, WIN), (q_ref, q_buf, 0))
    local = []
    for n, (src, dst, base) in enumerate(streams):
        local.append(
            pltpu.make_async_copy(src.at[0, :, block(h)], dst.at[rows(h, base)], local_sem.at[n])
        )
    local.append(pltpu.make_async_copy(fresh_gu_ref.at[0], fgu_buf, local_sem.at[3]))
    local.append(pltpu.make_async_copy(fresh_down_ref.at[0], fdown_buf, local_sem.at[4]))
    for copy in local:
        copy.start()

    pl.semaphore_wait(barrier, n_peer + 2)

    sends = []
    receives = {}

    def remote(name, src, dst, there, sem, here=None):
        copy = pltpu.make_async_remote_copy(
            src_ref=src, dst_ref=dst, send_sem=send_sem.at[sem], recv_sem=recv_sem.at[sem],
            device_id=there, device_id_type=MESH,
        )
        copy.start()
        sends.append(copy)
        arriving = copy if here is None else pltpu.make_async_remote_copy(
            src_ref=src, dst_ref=here, send_sem=send_sem.at[sem], recv_sem=recv_sem.at[sem],
            device_id=there, device_id_type=MESH,
        )
        receives.setdefault(name, []).append(arriving)

    sem = 0
    for n, (src, dst, base) in enumerate(streams):
        for out, back in zip(to_peer, from_peer):
            remote(
                "tokens", src.at[0, :, block(out)], dst.at[rows(h, base)], (c, out), sem,
                dst.at[rows(back, base)],
            )
            sem += 1
    remote("state", gu_ref.at[0, 0], gu_buf, (succ, h), sem)
    remote("state", down_ref.at[0, 0], down_buf, (succ, h), sem + 1)
    remote("tails", tail_k_ref, k_buf.at[pl.ds(0, WIN)], (succ, h), sem + 2)
    remote("tails", tail_v_ref, v_buf.at[pl.ds(0, WIN)], (succ, h), sem + 3)

    length = len_ref[0, c]
    linked = (seq_ref[1, c] == seq_ref[0, pred]).astype(jnp.int32)
    gain = gain_ref[...]
    exponent_scale = math.log2(math.e) / math.sqrt(HD)

    def attend(start):
        cols = WIN + TILE
        scores = nt(q_buf[pl.ds(start, TILE)], k_buf[pl.ds(start, cols)])
        key_pos = start - WIN + lax.broadcasted_iota(jnp.int32, (1, cols), 1)
        usable = jnp.where(key_pos < length, 1, 0) * jnp.where(key_pos >= 0, 1, linked)
        bias = jnp.where(usable > 0, 0.0, NEG)
        row = lax.broadcasted_iota(jnp.int32, (TILE, TILE), 0)
        col = lax.broadcasted_iota(jnp.int32, (TILE, TILE), 1)
        pieces = []
        for at in range(0, cols, TILE):
            own = scores[:, at : at + TILE]
            masked = own + bias[:, at : at + TILE]
            if at == 0:
                masked = jnp.where(col > row, masked, NEG)
            elif at == WIN:
                masked = jnp.where(col < row, masked, jnp.where(col == row, own, NEG))
            pieces.append(masked)
        scores = jnp.concatenate(pieces, axis=1)
        largest = jnp.max(scores, axis=-1, keepdims=True)
        exponent = jnp.exp2((scores - largest) * exponent_scale)
        total = jnp.sum(exponent, axis=-1, keepdims=True)
        weights = (exponent * (1.0 / total)).astype(jnp.bfloat16)
        return nn(weights, v_buf[pl.ds(start, cols)])

    for copy in local:
        copy.wait()
    for copy in receives["tokens"]:
        copy.wait_recv()
    for start in range(WIN, BLOCK, TILE):
        part_buf[pl.ds(start, TILE)] = attend(start)

    for copy in receives["state"]:
        copy.wait_recv()
    w_gate = jnp.where(linked > 0, gu_buf[0], fgu_buf[0])
    w_up = jnp.where(linked > 0, gu_buf[1], fgu_buf[1])
    w_down = jnp.where(linked > 0, down_buf[...], fdown_buf[...])
    down_high, down_low = split(w_down)
    gate_high, gate_low = split(w_gate)
    up_high, up_low = split(w_up)
    in_weights = jnp.concatenate(
        [
            jnp.concatenate([gate_high, up_high], axis=1),
            jnp.concatenate([gate_low, up_low], axis=1),
        ],
        axis=0,
    )
    out_weights = jnp.concatenate([down_high, down_low], axis=1)

    def fast(start):
        own = q_buf[pl.ds(start, TILE)]
        wide = own.astype(jnp.float32)
        unit = lax.rsqrt(jnp.mean(wide * wide, axis=-1, keepdims=True) + EPS)
        hidden = nn(jnp.concatenate([own, own], axis=1), in_weights) * unit
        gate, up = hidden[:, :HID], hidden[:, HID:]
        act_high, act_low = split(gate * sigmoid(gate) * up)
        both = nn(act_high, out_weights)
        result = both[:, :HD] + both[:, HD:] + nn(act_low, down_high)
        scale = lax.rsqrt(jnp.mean(result * result, axis=-1, keepdims=True) + EPS)
        return result * scale * gain

    def finish(start, value):
        live = (start + lax.broadcasted_iota(jnp.int32, (TILE, 1), 0)) < length
        out_buf[pl.ds(start, TILE)] = jnp.where(live, value, 0.0).astype(jnp.bfloat16)

    for start in range(WIN, BLOCK, TILE):
        finish(start, part_buf[pl.ds(start, TILE)] + fast(start))
    for start in range(0, WIN, TILE):
        part_buf[pl.ds(start, TILE)] = fast(start)

    for copy in receives["tails"]:
        copy.wait_recv()
    for start in range(0, WIN, TILE):
        finish(start, part_buf[pl.ds(start, TILE)] + attend(start))

    out_sends, out_receives = [], []
    own_part = pltpu.make_async_copy(
        out_buf.at[rows(h, 0)], mixed_ref.at[0, :, block(h)], local_sem.at[5]
    )
    for n, (out, back) in enumerate(zip(to_peer, from_peer)):
        copy = pltpu.make_async_remote_copy(
            src_ref=out_buf.at[rows(out, 0)], dst_ref=mixed_ref.at[0, :, block(h)],
            send_sem=out_send_sem.at[n], recv_sem=out_recv_sem.at[n],
            device_id=(c, out), device_id_type=MESH,
        )
        copy.start()
        out_sends.append(copy)
        out_receives.append(
            pltpu.make_async_remote_copy(
                src_ref=out_buf.at[rows(out, 0)], dst_ref=mixed_ref.at[0, :, block(back)],
                send_sem=out_send_sem.at[n], recv_sem=out_recv_sem.at[n],
                device_id=(c, out), device_id_type=MESH,
            )
        )
    own_part.start()

    key_weights = jnp.concatenate(
        [
            jnp.concatenate(split(w_gate.T), axis=1),
            jnp.concatenate(split(w_up.T), axis=1),
        ],
        axis=0,
    )
    ones = jnp.ones((8, 2 * HD), jnp.bfloat16)
    grad_in = jnp.zeros((2 * HID, HD), jnp.float32)
    grad_down = jnp.zeros((HID, HD), jnp.float32)
    for start in range(0, BLOCK, TILE):
        key = k_buf[pl.ds(WIN + start, TILE)]
        value = v_buf[pl.ds(WIN + start, TILE)]
        wide = key.astype(jnp.float32)
        squares = nt(ones, jnp.concatenate(split(wide * wide), axis=1))[0:1]
        unit = lax.rsqrt(squares * (1.0 / HD) + EPS)
        token = start + lax.broadcasted_iota(jnp.int32, (1, TILE), 1)
        rate = jnp.where(token < length, rate_ref[0, :, pl.ds(start, TILE)], 0.0)
        hidden = nt(key_weights, jnp.concatenate([key, key], axis=1)) * unit
        gate, up = hidden[:HID], hidden[HID:]
        s = sigmoid(gate)
        act = gate * s
        back = nt(out_weights, jnp.concatenate([value, value], axis=1)) * rate
        grad_down += nn((act * up * rate).astype(jnp.bfloat16), value)
        back = back * unit
        factor = jnp.concatenate([back * up * s * (1.0 + gate * (1.0 - s)), back * act], axis=0)
        grad_in += nn(factor.astype(jnp.bfloat16), key)

    def renormed(old, new):
        old_mean = jnp.mean(old * old, axis=0, keepdims=True) + EPS
        new_mean = jnp.mean(new * new, axis=0, keepdims=True) + EPS
        return new * (jnp.sqrt(old_mean) * lax.rsqrt(new_mean))

    gu_out_ref[0, 0, 0] = renormed(w_gate, w_gate + grad_in[:HID].T)
    gu_out_ref[0, 0, 1] = renormed(w_up, w_up + grad_in[HID:].T)
    down_out_ref[0, 0] = renormed(w_down, w_down + grad_down)

    own_part.wait()
    for copy in sends + out_sends:
        copy.wait_send()
    for copy in out_receives:
        copy.wait_recv()


def solution(mesh):
    ctx_count = mesh.shape["ctx"]
    n_remote = 3 * len(PEERS) + 4

    def on_device(
        queries, keys, values, rates, tail_keys, tail_values, state_in_gu, state_in_down,
        fresh_gu, fresh_down, out_gain, seq_ids, live_lengths,
    ):
        hbm = pl.BlockSpec(memory_space=pltpu.HBM)
        vmem = pl.BlockSpec(memory_space=pltpu.VMEM)
        smem = pl.BlockSpec(memory_space=pltpu.SMEM)

        def body(*refs):
            kernel(ctx_count, *refs)

        return pl.pallas_call(
            body,
            name="layer",
            out_shape=(
                jax.ShapeDtypeStruct(queries.shape, jnp.bfloat16),
                jax.ShapeDtypeStruct(state_in_gu.shape, jnp.float32),
                jax.ShapeDtypeStruct(state_in_down.shape, jnp.float32),
            ),
            in_specs=[hbm, hbm, hbm, vmem, hbm, hbm, hbm, hbm, hbm, hbm, vmem, smem, smem],
            out_specs=(vmem, vmem, vmem),
            scratch_shapes=[
                pltpu.VMEM((BLOCK, HD), jnp.bfloat16),
                pltpu.VMEM((WIN + BLOCK, HD), jnp.bfloat16),
                pltpu.VMEM((WIN + BLOCK, HD), jnp.bfloat16),
                pltpu.VMEM((2, HD, HID), jnp.float32),
                pltpu.VMEM((HID, HD), jnp.float32),
                pltpu.VMEM((2, HD, HID), jnp.float32),
                pltpu.VMEM((HID, HD), jnp.float32),
                pltpu.VMEM((BLOCK, HD), jnp.bfloat16),
                pltpu.VMEM((BLOCK, HD), jnp.float32),
                pltpu.SemaphoreType.DMA((6,)),
                pltpu.SemaphoreType.DMA((n_remote,)),
                pltpu.SemaphoreType.DMA((n_remote,)),
                pltpu.SemaphoreType.DMA((len(PEERS),)),
                pltpu.SemaphoreType.DMA((len(PEERS),)),
            ],
            compiler_params=pltpu.CompilerParams(
                collective_id=0, has_side_effects=True
            ),
        )(
            queries, keys, values, rates, tail_keys, tail_values, state_in_gu, state_in_down,
            fresh_gu, fresh_down, out_gain[None], seq_ids.T, live_lengths.T,
        )

    placed = (
        P(None, ("ctx", "head"), None),
        P(None, ("ctx", "head"), None),
        P(None, ("ctx", "head"), None),
        P(None, "head", "ctx"),
        P("ctx", "head"),
        P("ctx", "head"),
        P("ctx", "head", None, None, None),
        P("ctx", "head", None, None),
        P("head", None, None, None),
        P("head", None, None),
        P("head"),
        P(),
        P(),
    )
    return jax.shard_map(
        on_device,
        mesh=mesh,
        in_specs=placed,
        out_specs=(
            P(None, ("ctx", "head"), None),
            P("ctx", "head", None, None, None),
            P("ctx", "head", None, None),
        ),
        check_vma=False,
    )
```

time: 103 us -> 45.5 us (0.44)
  the two profiles are of different devices: /device:TPU:48 before, /device:TPU:2 now
where the time goes in v1:
time: 45.5 us; the launch traced here: 45.3 us
  Pallas kernels  41.3 us (91%)
  local copies, waits for them, and re-layouts  3.37 us (7%)
  between operations  0.65 us (1%)
    pallas_call x1, Pallas kernels, on_device(): pl.pallas_call(body, name='layer', out_shape=(jax.ShapeDtypeStruct(querie...  41.3 us
    unnamed x7, local copies, waits for them, and re-layouts  3.37 us

profile of v1, /device:TPU:2, one launch (start us, length us, event | category | flops | bytes accessed | tf_op | source)
XLA Modules:
  0.0 45.3 jit_solution(12421702466801093490)
XLA Ops:
  0.6 41.3 %layer.1 = (bf16[1,128,1024]{2,1,0:T(8,128)(2,1)}, f32[1,1,2,128,256]{4,3,2,1,0:T(8,128)}, f32[1,1,256,128]{3,2,1,0:T(8,128)}) custom-call(bf16[1,128,1024]{2,1,0:T(8,128)(2,1)} %refs_0_.1, bf16[1,128,1024]{2,1,0:T(8,128)(2,1)} %refs_1_.1, bf16[1,128,1024]{2,1,0:T(8,128)(2,1)} %refs_2_.1, f32[1,1,1024]{2,1,0:T(1,128)} %refs_3_.1, bf16[512,128]{1,0:T(8,128)(2,1)} %refs_4_.1, ...), custom_call_target="tpu_custom_call" | custom-call | tf_op jit(solution)/shard_map/layer/pallas_call | solution.py:275
  41.9 0.0 copy-start
  41.9 1.7 %copy.19 = bf16[1,128,1024]{2,1,0:T(8,128)(2,1)} copy(bf16[1,128,1024]{2,1,0:T(8,128)(2,1)} %get-tuple-element.6) | data formatting | bytes 524288
  43.7 0.0 copy-done
  43.7 0.0 copy-start.1
  43.7 0.7 %copy.20 = f32[1,1,2,128,256]{4,3,2,1,0:T(8,128)} copy(f32[1,1,2,128,256]{4,3,2,1,0:T(8,128)S(1)} %copy-done) | data formatting | bytes 524288
  44.4 0.3 copy-done.1
  44.7 0.7 %copy.21 = f32[1,1,256,128]{3,2,1,0:T(8,128)} copy(f32[1,1,256,128]{3,2,1,0:T(8,128)S(1)} %copy-done.1) | data formatting | bytes 262144
Async XLA Ops:
  41.9 1.7 %copy-start = (f32[1,1,2,128,256]{4,3,2,1,0:T(8,128)S(1)}, f32[1,1,2,128,256]{4,3,2,1,0:T(8,128)}, u32[]{:S(2)}) copy-start(f32[1,1,2,128,256]{4,3,2,1,0:T(8,128)} %get-tuple-element.7) | copy-start | bytes 786436
  43.7 1.0 %copy-start.1 = (f32[1,1,256,128]{3,2,1,0:T(8,128)S(1)}, f32[1,1,256,128]{3,2,1,0:T(8,128)}, u32[]{:S(2)}) copy-start(f32[1,1,256,128]{3,2,1,0:T(8,128)} %get-tuple-element.8) | copy-start | bytes 393220

commit v2 on v1

--- a/solution.py
+++ b/solution.py
@@ -17,6 +17,7 @@
 TILE = 256
 X_SIZE = 4
 Z_SIZE = 2
+STEPS = 32767.0
 PEERS = tuple((dx, dz) for dz in (1, 0) for dx in (2, 1, 3, 0) if (dx, dz) != (0, 0))
 
 
@@ -40,10 +41,12 @@
 
 def kernel(
     ctx_count,
-    q_ref, k_ref, v_ref, rate_ref, tail_k_ref, tail_v_ref, gu_ref, down_ref,
-    fresh_gu_ref, fresh_down_ref, gain_ref, seq_ref, len_ref,
+    q_ref, k_ref, v_ref, rates_ref, tail_k_ref, tail_v_ref, gu_ref, down_ref,
+    fresh_gu_ref, fresh_down_ref, gains_ref, seqs_ref, lens_ref,
     mixed_ref, gu_out_ref, down_out_ref,
     q_buf, k_buf, v_buf, gu_buf, down_buf, fgu_buf, fdown_buf, out_buf, part_buf,
+    gu_code, down_code, scale_code, gu_in, down_in, scale_in,
+    rate_ref, gain_ref, seq_ref, len_ref,
     local_sem, send_sem, recv_sem, out_send_sem, out_recv_sem,
 ):
     c = lax.axis_index("ctx")
@@ -62,8 +65,7 @@
     barrier = pltpu.get_barrier_semaphore()
     for peer in to_peer:
         pl.semaphore_signal(barrier, inc=1, device_id=(c, peer), device_id_type=MESH)
-    for other in (succ, pred):
-        pl.semaphore_signal(barrier, inc=1, device_id=(other, h), device_id_type=MESH)
+    pl.semaphore_signal(barrier, inc=1, device_id=(pred, h), device_id_type=MESH)
 
     def block(index):
         return pl.ds(pl.multiple_of(index * HD, HD), HD)
@@ -72,47 +74,87 @@
         return pl.ds(pl.multiple_of(base + index * HD, HD), HD)
 
     streams = ((k_ref, k_buf, WIN), (v_ref, v_buf, WIN), (q_ref, q_buf, 0))
-    local = []
-    for n, (src, dst, base) in enumerate(streams):
-        local.append(
-            pltpu.make_async_copy(src.at[0, :, block(h)], dst.at[rows(h, base)], local_sem.at[n])
+    early = [
+        pltpu.make_async_copy(gu_ref.at[0, 0], gu_buf, local_sem.at[0]),
+        pltpu.make_async_copy(down_ref.at[0, 0], down_buf, local_sem.at[1]),
+    ]
+    local = [
+        pltpu.make_async_copy(src.at[0, :, block(h)], dst.at[rows(h, base)], local_sem.at[2 + n])
+        for n, (src, dst, base) in enumerate(streams)
+    ]
+    local += [
+        pltpu.make_async_copy(src, dst, local_sem.at[5 + n])
+        for n, (src, dst) in enumerate(
+            (
+                (fresh_gu_ref.at[0], fgu_buf),
+                (fresh_down_ref.at[0], fdown_buf),
+                (rates_ref.at[0], rate_ref),
+                (gains_ref, gain_ref),
+                (seqs_ref, seq_ref),
+                (lens_ref, len_ref),
+            )
         )
-    local.append(pltpu.make_async_copy(fresh_gu_ref.at[0], fgu_buf, local_sem.at[3]))
-    local.append(pltpu.make_async_copy(fresh_down_ref.at[0], fdown_buf, local_sem.at[4]))
-    for copy in local:
+    ]
+    for copy in early + local:
         copy.start()
-
-    pl.semaphore_wait(barrier, n_peer + 2)
-
-    sends = []
+    for copy in early:
+        copy.wait()
+
+    def encode(matrix, code, row):
+        largest = jnp.maximum(jnp.max(jnp.abs(matrix), axis=0, keepdims=True), 1e-30)
+        code[...] = jnp.round(matrix * (STEPS / largest)).astype(jnp.int32).astype(jnp.int16)
+        scale_code[row : row + 1, : matrix.shape[1]] = largest * (1.0 / STEPS)
+
+    def decode(code, row):
+        return code.astype(jnp.int32).astype(jnp.float32) * scale_in[row : row + 1, : code.shape[1]]
+
+    scale_code[...] = jnp.zeros_like(scale_code)
+    encode(gu_buf[0], gu_code.at[0], 0)
+    encode(gu_buf[1], gu_code.at[1], 1)
+    encode(down_buf[...], down_code, 2)
+
+    pl.semaphore_wait(barrier, n_peer + 1)
+
     receives = {}
-
-    def remote(name, src, dst, there, sem, here=None):
-        copy = pltpu.make_async_remote_copy(
-            src_ref=src, dst_ref=dst, send_sem=send_sem.at[sem], recv_sem=recv_sem.at[sem],
-            device_id=there, device_id_type=MESH,
-        )
-        copy.start()
-        sends.append(copy)
-        arriving = copy if here is None else pltpu.make_async_remote_copy(
-            src_ref=src, dst_ref=here, send_sem=send_sem.at[sem], recv_sem=recv_sem.at[sem],
-            device_id=there, device_id_type=MESH,
-        )
-        receives.setdefault(name, []).append(arriving)
+    token_sends, ctx_sends = [], []
+
+    def remote(name, group, src, dst, there, sem, here):
+        def describe(at):
+            return pltpu.make_async_remote_copy(
+                src_ref=src, dst_ref=at, send_sem=send_sem.at[sem], recv_sem=recv_sem.at[sem],
+                device_id=there, device_id_type=MESH,
+            )
+
+        group.append(describe(dst))
+        receives.setdefault(name, []).append(describe(here))
 
     sem = 0
     for n, (src, dst, base) in enumerate(streams):
         for out, back in zip(to_peer, from_peer):
             remote(
-                "tokens", src.at[0, :, block(out)], dst.at[rows(h, base)], (c, out), sem,
+                "tokens", token_sends, src.at[0, :, block(out)], dst.at[rows(h, base)], (c, out), sem,
                 dst.at[rows(back, base)],
             )
             sem += 1
-    remote("state", gu_ref.at[0, 0], gu_buf, (succ, h), sem)
-    remote("state", down_ref.at[0, 0], down_buf, (succ, h), sem + 1)
-    remote("tails", tail_k_ref, k_buf.at[pl.ds(0, WIN)], (succ, h), sem + 2)
-    remote("tails", tail_v_ref, v_buf.at[pl.ds(0, WIN)], (succ, h), sem + 3)
-
+    recent, older = pl.ds(WIN // 2, WIN // 2), pl.ds(0, WIN // 2)
+    for name, src, dst in (
+        ("state", scale_code, scale_in),
+        ("state", gu_code, gu_in),
+        ("state", down_code, down_in),
+        ("recent", tail_k_ref.at[recent], k_buf.at[recent]),
+        ("recent", tail_v_ref.at[recent], v_buf.at[recent]),
+        ("older", tail_k_ref.at[older], k_buf.at[older]),
+        ("older", tail_v_ref.at[older], v_buf.at[older]),
+    ):
+        remote(name, ctx_sends, src, dst, (succ, h), sem, dst)
+        sem += 1
+    sends = token_sends + ctx_sends
+
+    for copy in sends:
+        copy.start()
+
+    for copy in local:
+        copy.wait()
     length = len_ref[0, c]
     linked = (seq_ref[1, c] == seq_ref[0, pred]).astype(jnp.int32)
     gain = gain_ref[...]
@@ -142,8 +184,6 @@
         weights = (exponent * (1.0 / total)).astype(jnp.bfloat16)
         return nn(weights, v_buf[pl.ds(start, cols)])
 
-    for copy in local:
-        copy.wait()
     for copy in receives["tokens"]:
         copy.wait_recv()
     for start in range(WIN, BLOCK, TILE):
@@ -151,9 +191,9 @@
 
     for copy in receives["state"]:
         copy.wait_recv()
-    w_gate = jnp.where(linked > 0, gu_buf[0], fgu_buf[0])
-    w_up = jnp.where(linked > 0, gu_buf[1], fgu_buf[1])
-    w_down = jnp.where(linked > 0, down_buf[...], fdown_buf[...])
+    w_gate = jnp.where(linked > 0, decode(gu_in[0], 0), fgu_buf[0])
+    w_up = jnp.where(linked > 0, decode(gu_in[1], 1), fgu_buf[1])
+    w_down = jnp.where(linked > 0, decode(down_in[...], 2), fdown_buf[...])
     down_high, down_low = split(w_down)
     gate_high, gate_low = split(w_gate)
     up_high, up_low = split(w_up)
@@ -187,31 +227,42 @@
     for start in range(0, WIN, TILE):
         part_buf[pl.ds(start, TILE)] = fast(start)
 
-    for copy in receives["tails"]:
-        copy.wait_recv()
-    for start in range(0, WIN, TILE):
-        finish(start, part_buf[pl.ds(start, TILE)] + attend(start))
-
-    out_sends, out_receives = [], []
-    own_part = pltpu.make_async_copy(
-        out_buf.at[rows(h, 0)], mixed_ref.at[0, :, block(h)], local_sem.at[5]
-    )
-    for n, (out, back) in enumerate(zip(to_peer, from_peer)):
-        copy = pltpu.make_async_remote_copy(
+    out_receives = [
+        pltpu.make_async_remote_copy(
+            src_ref=out_buf.at[rows(out, 0)], dst_ref=mixed_ref.at[0, :, block(back)],
+            send_sem=out_send_sem.at[n], recv_sem=out_recv_sem.at[n],
+            device_id=(c, out), device_id_type=MESH,
+        )
+        for n, (out, back) in enumerate(zip(to_peer, from_peer))
+    ]
+    out_sends = [
+        pltpu.make_async_remote_copy(
             src_ref=out_buf.at[rows(out, 0)], dst_ref=mixed_ref.at[0, :, block(h)],
             send_sem=out_send_sem.at[n], recv_sem=out_recv_sem.at[n],
             device_id=(c, out), device_id_type=MESH,
         )
-        copy.start()
-        out_sends.append(copy)
-        out_receives.append(
-            pltpu.make_async_remote_copy(
-                src_ref=out_buf.at[rows(out, 0)], dst_ref=mixed_ref.at[0, :, block(back)],
-                send_sem=out_send_sem.at[n], recv_sem=out_recv_sem.at[n],
-                device_id=(c, out), device_id_type=MESH,
-            )
-        )
-    own_part.start()
+        for n, out in enumerate(to_peer)
+    ]
+    own_part = pltpu.make_async_copy(
+        out_buf.at[rows(h, 0)], mixed_ref.at[0, :, block(h)], local_sem.at[0]
+    )
+
+    def send_rows(start, stop):
+        for copy, out in [*zip(out_sends, to_peer), (own_part, h)]:
+            @pl.when((out >= start // HD) & (out < stop // HD))
+            def _():
+                copy.start()
+
+    send_rows(WIN, BLOCK)
+
+    for copy in receives["recent"]:
+        copy.wait_recv()
+    finish(TILE, part_buf[pl.ds(TILE, TILE)] + attend(TILE))
+    send_rows(TILE, WIN)
+    for copy in receives["older"]:
+        copy.wait_recv()
+    finish(0, part_buf[pl.ds(0, TILE)] + attend(0))
+    send_rows(0, TILE)
 
     key_weights = jnp.concatenate(
         [
@@ -230,7 +281,7 @@
         squares = nt(ones, jnp.concatenate(split(wide * wide), axis=1))[0:1]
         unit = lax.rsqrt(squares * (1.0 / HD) + EPS)
         token = start + lax.broadcasted_iota(jnp.int32, (1, TILE), 1)
-        rate = jnp.where(token < length, rate_ref[0, :, pl.ds(start, TILE)], 0.0)
+        rate = jnp.where(token < length, rate_ref[:, pl.ds(start, TILE)], 0.0)
         hidden = nt(key_weights, jnp.concatenate([key, key], axis=1)) * unit
         gate, up = hidden[:HID], hidden[HID:]
         s = sigmoid(gate)
@@ -259,7 +310,7 @@
 
 def solution(mesh):
     ctx_count = mesh.shape["ctx"]
-    n_remote = 3 * len(PEERS) + 4
+    n_remote = 3 * len(PEERS) + 7
 
     def on_device(
         queries, keys, values, rates, tail_keys, tail_values, state_in_gu, state_in_down,
@@ -267,12 +318,11 @@
     ):
         hbm = pl.BlockSpec(memory_space=pltpu.HBM)
         vmem = pl.BlockSpec(memory_space=pltpu.VMEM)
-        smem = pl.BlockSpec(memory_space=pltpu.SMEM)
 
         def body(*refs):
             kernel(ctx_count, *refs)
 
-        return pl.pallas_call(
+        results = pl.pallas_call(
             body,
             name="layer",
             out_shape=(
@@ -280,7 +330,7 @@
                 jax.ShapeDtypeStruct(state_in_gu.shape, jnp.float32),
                 jax.ShapeDtypeStruct(state_in_down.shape, jnp.float32),
             ),
-            in_specs=[hbm, hbm, hbm, vmem, hbm, hbm, hbm, hbm, hbm, hbm, vmem, smem, smem],
+            in_specs=[hbm] * 13,
             out_specs=(vmem, vmem, vmem),
             scratch_shapes=[
                 pltpu.VMEM((BLOCK, HD), jnp.bfloat16),
@@ -292,19 +342,53 @@
                 pltpu.VMEM((HID, HD), jnp.float32),
                 pltpu.VMEM((BLOCK, HD), jnp.bfloat16),
                 pltpu.VMEM((BLOCK, HD), jnp.float32),
-                pltpu.SemaphoreType.DMA((6,)),
+                pltpu.VMEM((2, HD, HID), jnp.int16),
+                pltpu.VMEM((HID, HD), jnp.int16),
+                pltpu.VMEM((8, HID), jnp.float32),
+                pltpu.VMEM((2, HD, HID), jnp.int16),
+                pltpu.VMEM((HID, HD), jnp.int16),
+                pltpu.VMEM((8, HID), jnp.float32),
+                pltpu.VMEM((1, BLOCK), jnp.float32),
+                pltpu.VMEM((1, HD), jnp.float32),
+                pltpu.SMEM((2, ctx_count), jnp.int32),
+                pltpu.SMEM((1, ctx_count), jnp.int32),
+                pltpu.SemaphoreType.DMA((11,)),
                 pltpu.SemaphoreType.DMA((n_remote,)),
                 pltpu.SemaphoreType.DMA((n_remote,)),
                 pltpu.SemaphoreType.DMA((len(PEERS),)),
                 pltpu.SemaphoreType.DMA((len(PEERS),)),
             ],
             compiler_params=pltpu.CompilerParams(
-                collective_id=0, has_side_effects=True
+                collective_id=0, has_side_effects=True, vmem_limit_bytes=40 * 1024 * 1024
             ),
         )(
-            queries, keys, values, rates, tail_keys, tail_values, state_in_gu, state_in_down,
-            fresh_gu, fresh_down, out_gain[None], seq_ids.T, live_lengths.T,
+            *[
+                pltpu.with_memory_space_constraint(array, pltpu.HBM)
+                for array in (
+                    queries, keys, values, rates, tail_keys, tail_values, state_in_gu, state_in_down,
+                    fresh_gu, fresh_down, out_gain[None], seq_ids.T, live_lengths.T,
+                )
+            ]
         )
+
+        def store(*refs):
+            copies = [
+                pltpu.make_async_copy(refs[n], refs[n + 3], refs[6].at[n]) for n in range(3)
+            ]
+            for copy in copies:
+                copy.start()
+            for copy in copies:
+                copy.wait()
+
+        return pl.pallas_call(
+            store,
+            name="store",
+            out_shape=tuple(jax.ShapeDtypeStruct(r.shape, r.dtype) for r in results),
+            in_specs=[vmem] * 3,
+            out_specs=[hbm] * 3,
+            scratch_shapes=[pltpu.SemaphoreType.DMA((3,))],
+            compiler_params=pltpu.CompilerParams(vmem_limit_bytes=8 * 1024 * 1024),
+        )(*results)
 
     placed = (
         P(None, ("ctx", "head"), None),

time: 45.5 us -> 35.8 us (0.79)
  the two profiles are of different devices: /device:TPU:2 before, /device:TPU:384 now
where the time goes in v2:
time: 35.8 us; the launch traced here: 35.6 us
  Pallas kernels  35 us (98%)
  between operations  0.64 us (2%)
    pallas_call x1, Pallas kernels, on_device(): pl.pallas_call(body, name='layer', out_shape=(jax.ShapeDtypeStruct(querie...  34.1 us
    pallas_call x1, Pallas kernels, on_device(): pl.pallas_call(store, name='store', out_shape=tuple((jax.ShapeDtypeStruct...  0.86 us

profile of v2, /device:TPU:384, one launch (start us, length us, event | category | flops | bytes accessed | tf_op | source)
XLA Modules:
  0.0 35.6 jit_solution(3423357345980786478)
XLA Ops:
  0.6 34.1 %layer.1 = (bf16[1,128,1024]{2,1,0:T(8,128)(2,1)S(1)}, f32[1,1,2,128,256]{4,3,2,1,0:T(8,128)S(1)}, f32[1,1,256,128]{3,2,1,0:T(8,128)S(1)}) custom-call(bf16[1,128,1024]{2,1,0:T(8,128)(2,1)} %refs_0_.1, bf16[1,128,1024]{2,1,0:T(8,128)(2,1)} %refs_1_.1, bf16[1,128,1024]{2,1,0:T(8,128)(2,1)} %refs_2_.1, f32[1,1,1024]{2,1,0:T(1,128)} %refs_3_.1, ...), custom_call_target="tpu_custom_call" | custom-call | tf_op jit(solution)/shard_map/layer/pallas_call | solution.py:325
  34.8 0.9 %store.1 = (bf16[1,128,1024]{2,1,0:T(8,128)(2,1)}, f32[1,1,2,128,256]{4,3,2,1,0:T(8,128)}, f32[1,1,256,128]{3,2,1,0:T(8,128)}) custom-call(bf16[1,128,1024]{2,1,0:T(8,128)(2,1)S(1)} %get-tuple-element.6.refs_0_, f32[1,1,2,128,256]{4,3,2,1,0:T(8,128)S(1)} %get-tuple-element.7.refs_1_, f32[1,1,256,128]{3,2,1,0:T(8,128)S(1)} %get-tuple-element.8.refs_2_), custom_call_target="tpu_custom_call" | custom-call | tf_op jit(solution)/shard_map/store/pallas_call | solution.py:383

commit v3 on v2

--- a/solution.py
+++ b/solution.py
@@ -17,6 +17,7 @@
 TILE = 256
 X_SIZE = 4
 Z_SIZE = 2
+ROW = 8
 STEPS = 32767.0
 PEERS = tuple((dx, dz) for dz in (1, 0) for dx in (2, 1, 3, 0) if (dx, dz) != (0, 0))
 
@@ -46,8 +47,8 @@
     mixed_ref, gu_out_ref, down_out_ref,
     q_buf, k_buf, v_buf, gu_buf, down_buf, fgu_buf, fdown_buf, out_buf, part_buf,
     gu_code, down_code, scale_code, gu_in, down_in, scale_in,
-    rate_ref, gain_ref, seq_ref, len_ref,
-    local_sem, send_sem, recv_sem, out_send_sem, out_recv_sem,
+    rate_ref, gain_ref, seq_ref, len_ref, relay_buf,
+    local_sem, send_sem, recv_sem, out_send_sem, out_recv_sem, relay_send_sem, relay_recv_sem,
 ):
     c = lax.axis_index("ctx")
     h = lax.axis_index("head")
@@ -66,6 +67,24 @@
     for peer in to_peer:
         pl.semaphore_signal(barrier, inc=1, device_id=(c, peer), device_id_type=MESH)
     pl.semaphore_signal(barrier, inc=1, device_id=(pred, h), device_id_type=MESH)
+    at_row = lax.rem(c, ROW)
+    row = c - at_row
+    origin = (at_row == ROW - 1) & (hz == 0)
+    middle = (at_row == 3) & (hz == 1)
+    final = (at_row == 0) & (hz == 0)
+    middle_id = (row + 3, h + 1)
+    final_id = (lax.rem(row + ROW, ctx_count), h - 1)
+
+    @pl.when(final)
+    def _():
+        there = (lax.rem(row + ctx_count - ROW, ctx_count) + 3, h + 1)
+        pl.semaphore_signal(barrier, inc=1, device_id=there, device_id_type=MESH)
+
+    @pl.when(middle)
+    def _():
+        there = (row + ROW - 1, h - 1)
+        pl.semaphore_signal(barrier, inc=1, device_id=there, device_id_type=MESH)
+
 
     def block(index):
         return pl.ds(pl.multiple_of(index * HD, HD), HD)
@@ -113,7 +132,14 @@
     encode(gu_buf[1], gu_code.at[1], 1)
     encode(down_buf[...], down_code, 2)
 
-    pl.semaphore_wait(barrier, n_peer + 1)
+    @pl.when(origin | middle)
+    def _():
+        pl.semaphore_wait(barrier, n_peer + 2)
+
+    @pl.when(jnp.logical_not(origin | middle))
+    def _():
+        pl.semaphore_wait(barrier, n_peer + 1)
+
 
     receives = {}
     token_sends, ctx_sends = [], []
@@ -149,9 +175,48 @@
         remote(name, ctx_sends, src, dst, (succ, h), sem, dst)
         sem += 1
     sends = token_sends + ctx_sends
-
-    for copy in sends:
+    tail_sends = ctx_sends[3:]
+    detours, forwards = [], []
+    for n, (src, dst) in enumerate(
+        (
+            (tail_k_ref.at[recent], k_buf.at[recent]),
+            (tail_v_ref.at[recent], v_buf.at[recent]),
+            (tail_k_ref.at[older], k_buf.at[older]),
+            (tail_v_ref.at[older], v_buf.at[older]),
+        )
+    ):
+        at = sem - 4 + n
+        detours.append(
+            pltpu.make_async_remote_copy(
+                src_ref=src, dst_ref=relay_buf.at[n], send_sem=send_sem.at[at],
+                recv_sem=relay_recv_sem.at[n], device_id=middle_id, device_id_type=MESH,
+            )
+        )
+        forwards.append(
+            pltpu.make_async_remote_copy(
+                src_ref=relay_buf.at[n], dst_ref=dst, send_sem=relay_send_sem.at[n],
+                recv_sem=recv_sem.at[at], device_id=final_id, device_id_type=MESH,
+            )
+        )
+
+    @pl.when(origin)
+    def _():
+        for copy in detours:
+            copy.start()
+
+    for copy in token_sends + ctx_sends[:3]:
         copy.start()
+
+    @pl.when(jnp.logical_not(origin))
+    def _():
+        for copy in tail_sends:
+            copy.start()
+
+    @pl.when(middle)
+    def _():
+        for arriving, copy in zip(detours, forwards):
+            arriving.wait_recv()
+            copy.start()
 
     for copy in local:
         copy.wait()
@@ -302,6 +367,12 @@
     down_out_ref[0, 0] = renormed(w_down, w_down + grad_down)
 
     own_part.wait()
+
+    @pl.when(middle)
+    def _():
+        for copy in forwards:
+            copy.wait_send()
+
     for copy in sends + out_sends:
         copy.wait_send()
     for copy in out_receives:
@@ -352,11 +423,14 @@
                 pltpu.VMEM((1, HD), jnp.float32),
                 pltpu.SMEM((2, ctx_count), jnp.int32),
                 pltpu.SMEM((1, ctx_count), jnp.int32),
+                pltpu.VMEM((4, WIN // 2, HD), jnp.bfloat16),
                 pltpu.SemaphoreType.DMA((11,)),
                 pltpu.SemaphoreType.DMA((n_remote,)),
                 pltpu.SemaphoreType.DMA((n_remote,)),
                 pltpu.SemaphoreType.DMA((len(PEERS),)),
                 pltpu.SemaphoreType.DMA((len(PEERS),)),
+                pltpu.SemaphoreType.DMA((4,)),
+                pltpu.SemaphoreType.DMA((4,)),
             ],
             compiler_params=pltpu.CompilerParams(
                 collective_id=0, has_side_effects=True, vmem_limit_bytes=40 * 1024 * 1024

time: 35.8 us -> 33.2 us (0.927)
  the two profiles are of different devices: /device:TPU:384 before, /device:TPU:64 now
where the time goes in v3:
time: 33.2 us; the launch traced here: 33 us
  Pallas kernels  32.4 us (98%)
  between operations  0.64 us (2%)
    pallas_call x1, Pallas kernels, on_device(): pl.pallas_call(body, name='layer', out_shape=(jax.ShapeDtypeStruct(querie...  31.5 us
    pallas_call x1, Pallas kernels, on_device(): pl.pallas_call(store, name='store', out_shape=tuple((jax.ShapeDtypeStruct...  0.86 us

profile of v3, /device:TPU:64, one launch (start us, length us, event | category | flops | bytes accessed | tf_op | source)
XLA Modules:
  0.0 33.0 jit_solution(9201358996326546118)
XLA Ops:
  0.6 31.5 %layer.1 = (bf16[1,128,1024]{2,1,0:T(8,128)(2,1)S(1)}, f32[1,1,2,128,256]{4,3,2,1,0:T(8,128)S(1)}, f32[1,1,256,128]{3,2,1,0:T(8,128)S(1)}) custom-call(bf16[1,128,1024]{2,1,0:T(8,128)(2,1)} %refs_0_.1, bf16[1,128,1024]{2,1,0:T(8,128)(2,1)} %refs_1_.1, bf16[1,128,1024]{2,1,0:T(8,128)(2,1)} %refs_2_.1, f32[1,1,1024]{2,1,0:T(1,128)} %refs_3_.1, ...), custom_call_target="tpu_custom_call" | custom-call | tf_op jit(solution)/shard_map/layer/pallas_call | solution.py:396
  32.2 0.9 %store.1 = (bf16[1,128,1024]{2,1,0:T(8,128)(2,1)}, f32[1,1,2,128,256]{4,3,2,1,0:T(8,128)}, f32[1,1,256,128]{3,2,1,0:T(8,128)}) custom-call(bf16[1,128,1024]{2,1,0:T(8,128)(2,1)S(1)} %get-tuple-element.6.refs_0_, f32[1,1,2,128,256]{4,3,2,1,0:T(8,128)S(1)} %get-tuple-element.7.refs_1_, f32[1,1,256,128]{3,2,1,0:T(8,128)S(1)} %get-tuple-element.8.refs_2_), custom_call_target="tpu_custom_call" | custom-call | tf_op jit(solution)/shard_map/store/pallas_call | solution.py:457

commit v4 on v3

--- a/solution.py
+++ b/solution.py
@@ -17,6 +17,7 @@
 TILE = 256
 X_SIZE = 4
 Z_SIZE = 2
+PLAN = (2, 1, 2, 1, 1, 1, 0, 0)
 ROW = 8
 STEPS = 32767.0
 PEERS = tuple((dx, dz) for dz in (1, 0) for dx in (2, 1, 3, 0) if (dx, dz) != (0, 0))
@@ -155,13 +156,16 @@
         receives.setdefault(name, []).append(describe(here))
 
     sem = 0
-    for n, (src, dst, base) in enumerate(streams):
-        for out, back in zip(to_peer, from_peer):
-            remote(
-                "tokens", token_sends, src.at[0, :, block(out)], dst.at[rows(h, base)], (c, out), sem,
-                dst.at[rows(back, base)],
-            )
-            sem += 1
+    for dz in (1, 0):
+        for src, dst, base in streams:
+            for n in range(n_peer):
+                if PEERS[n][1] == dz:
+                    out, back = to_peer[n], from_peer[n]
+                    remote(
+                        "tokens", token_sends, src.at[0, :, block(out)], dst.at[rows(h, base)],
+                        (c, out), sem, dst.at[rows(back, base)],
+                    )
+                    sem += 1
     recent, older = pl.ds(WIN // 2, WIN // 2), pl.ds(0, WIN // 2)
     for name, src, dst in (
         ("state", scale_code, scale_in),
@@ -174,7 +178,7 @@
     ):
         remote(name, ctx_sends, src, dst, (succ, h), sem, dst)
         sem += 1
-    sends = token_sends + ctx_sends
+    sends = token_sends[3 * X_SIZE :] + ctx_sends
     tail_sends = ctx_sends[3:]
     detours, forwards = [], []
     for n, (src, dst) in enumerate(
@@ -199,18 +203,49 @@
             )
         )
 
+    far = lax.rem(c, 2) == 1
+    z = (at_row // 2) * Z_SIZE + hz
+
+    def chosen(stage):
+        picked = c < 0 if stage else jnp.logical_not(far)
+        for at, planned in enumerate(PLAN):
+            if planned == stage:
+                picked = picked | ((z == at) & far)
+        return picked
+
+    def start_ctx(stage):
+        when = chosen(stage)
+
+        @pl.when(when)
+        def _():
+            for copy in ctx_sends[:3]:
+                copy.start()
+
+        @pl.when(when & jnp.logical_not(origin))
+        def _():
+            for copy in tail_sends:
+                copy.start()
+
+    crossing = token_sends[: 3 * X_SIZE]
+    waits = chosen(2)
+
+    def drain(when):
+        @pl.when(when)
+        def _():
+            for copy in crossing:
+                copy.wait_send()
+
     @pl.when(origin)
     def _():
         for copy in detours:
             copy.start()
 
-    for copy in token_sends + ctx_sends[:3]:
+    start_ctx(0)
+    for copy in token_sends:
         copy.start()
-
-    @pl.when(jnp.logical_not(origin))
-    def _():
-        for copy in tail_sends:
-            copy.start()
+    start_ctx(1)
+    drain(waits)
+    start_ctx(2)
 
     @pl.when(middle)
     def _():
@@ -251,6 +286,7 @@
 
     for copy in receives["tokens"]:
         copy.wait_recv()
+    start_ctx(3)
     for start in range(WIN, BLOCK, TILE):
         part_buf[pl.ds(start, TILE)] = attend(start)
 
@@ -287,11 +323,6 @@
         live = (start + lax.broadcasted_iota(jnp.int32, (TILE, 1), 0)) < length
         out_buf[pl.ds(start, TILE)] = jnp.where(live, value, 0.0).astype(jnp.bfloat16)
 
-    for start in range(WIN, BLOCK, TILE):
-        finish(start, part_buf[pl.ds(start, TILE)] + fast(start))
-    for start in range(0, WIN, TILE):
-        part_buf[pl.ds(start, TILE)] = fast(start)
-
     out_receives = [
         pltpu.make_async_remote_copy(
             src_ref=out_buf.at[rows(out, 0)], dst_ref=mixed_ref.at[0, :, block(back)],
@@ -318,16 +349,38 @@
             def _():
                 copy.start()
 
-    send_rows(WIN, BLOCK)
-
-    for copy in receives["recent"]:
-        copy.wait_recv()
-    finish(TILE, part_buf[pl.ds(TILE, TILE)] + attend(TILE))
-    send_rows(TILE, WIN)
-    for copy in receives["older"]:
-        copy.wait_recv()
-    finish(0, part_buf[pl.ds(0, TILE)] + attend(0))
-    send_rows(0, TILE)
+    def first_rows_fast():
+        for start in range(0, WIN, TILE):
+            part_buf[pl.ds(start, TILE)] = fast(start)
+
+    def first_rows(start):
+        finish(start, part_buf[pl.ds(start, TILE)] + attend(start))
+        send_rows(start, start + TILE)
+
+    def last_rows():
+        for start in range(WIN, BLOCK, TILE):
+            finish(start, part_buf[pl.ds(start, TILE)] + fast(start))
+        send_rows(WIN, BLOCK)
+
+    @pl.when(hz == 0)
+    def _():
+        last_rows()
+        first_rows_fast()
+        for copy in receives["recent"]:
+            copy.wait_recv()
+        first_rows(TILE)
+        for copy in receives["older"]:
+            copy.wait_recv()
+        first_rows(0)
+
+    @pl.when(hz != 0)
+    def _():
+        first_rows_fast()
+        for copy in receives["recent"] + receives["older"]:
+            copy.wait_recv()
+        first_rows(0)
+        first_rows(TILE)
+        last_rows()
 
     key_weights = jnp.concatenate(
         [
@@ -367,6 +420,7 @@
     down_out_ref[0, 0] = renormed(w_down, w_down + grad_down)
 
     own_part.wait()
+    drain(jnp.logical_not(waits))
 
     @pl.when(middle)
     def _():

time: 33.2 us -> 33 us (level)
  the two profiles are of different devices: /device:TPU:64 before, /device:TPU:128 now
where the time goes in v4:
time: 33 us; the launch traced here: 32.8 us
  Pallas kernels  32.2 us (98%)
  between operations  0.64 us (2%)
    pallas_call x1, Pallas kernels, on_device(): pl.pallas_call(body, name='layer', out_shape=(jax.ShapeDtypeStruct(querie...  31.3 us
    pallas_call x1, Pallas kernels, on_device(): pl.pallas_call(store, name='store', out_shape=tuple((jax.ShapeDtypeStruct...  0.86 us

profile of v4, /device:TPU:128, one launch (start us, length us, event | category | flops | bytes accessed | tf_op | source)
XLA Modules:
  0.0 32.8 jit_solution(14948906195521961730)
XLA Ops:
  0.6 31.3 %layer.1 = (bf16[1,128,1024]{2,1,0:T(8,128)(2,1)S(1)}, f32[1,1,2,128,256]{4,3,2,1,0:T(8,128)S(1)}, f32[1,1,256,128]{3,2,1,0:T(8,128)S(1)}) custom-call(bf16[1,128,1024]{2,1,0:T(8,128)(2,1)} %refs_0_.1, bf16[1,128,1024]{2,1,0:T(8,128)(2,1)} %refs_1_.1, bf16[1,128,1024]{2,1,0:T(8,128)(2,1)} %refs_2_.1, f32[1,1,1024]{2,1,0:T(1,128)} %refs_3_.1, ...), custom_call_target="tpu_custom_call" | custom-call | tf_op jit(solution)/shard_map/layer/pallas_call | solution.py:450
  32.0 0.9 %store.1 = (bf16[1,128,1024]{2,1,0:T(8,128)(2,1)}, f32[1,1,2,128,256]{4,3,2,1,0:T(8,128)}, f32[1,1,256,128]{3,2,1,0:T(8,128)}) custom-call(bf16[1,128,1024]{2,1,0:T(8,128)(2,1)S(1)} %get-tuple-element.6.refs_0_, f32[1,1,2,128,256]{4,3,2,1,0:T(8,128)S(1)} %get-tuple-element.7.refs_1_, f32[1,1,256,128]{3,2,1,0:T(8,128)S(1)} %get-tuple-element.8.refs_2_), custom_call_target="tpu_custom_call" | custom-call | tf_op jit(solution)/shard_map/store/pallas_call | solution.py:511

commit v5 on v4

--- a/solution.py
+++ b/solution.py
@@ -500,9 +500,17 @@
         )
 
         def store(*refs):
-            copies = [
-                pltpu.make_async_copy(refs[n], refs[n + 3], refs[6].at[n]) for n in range(3)
+            mixed, pair, down, mixed_out, pair_out, down_out, sem = refs
+            parts = [
+                (mixed.at[0, pl.ds(at, 32)], mixed_out.at[0, pl.ds(at, 32)]) for at in range(0, HD, 32)
             ]
+            for at in range(0, HD, HD // 2):
+                for n in range(2):
+                    cut = pl.ds(at, HD // 2)
+                    parts.append((pair.at[0, 0, n, cut], pair_out.at[0, 0, n, cut]))
+            for at in range(0, HID, HD):
+                parts.append((down.at[0, 0, pl.ds(at, HD)], down_out.at[0, 0, pl.ds(at, HD)]))
+            copies = [pltpu.make_async_copy(a, b, sem.at[n]) for n, (a, b) in enumerate(parts)]
             for copy in copies:
                 copy.start()
             for copy in copies:
@@ -514,7 +522,7 @@
             out_shape=tuple(jax.ShapeDtypeStruct(r.shape, r.dtype) for r in results),
             in_specs=[vmem] * 3,
             out_specs=[hbm] * 3,
-            scratch_shapes=[pltpu.SemaphoreType.DMA((3,))],
+            scratch_shapes=[pltpu.SemaphoreType.DMA((10,))],
             compiler_params=pltpu.CompilerParams(vmem_limit_bytes=8 * 1024 * 1024),
         )(*results)
 

time: 33 us -> 33 us (level)
  no operation moved by 1% of the time
where the time goes in v5:
time: 33 us; the launch traced here: 32.9 us
  Pallas kernels  32.2 us (98%)
  between operations  0.64 us (2%)
    pallas_call x1, Pallas kernels, on_device(): pl.pallas_call(body, name='layer', out_shape=(jax.ShapeDtypeStruct(querie...  31.3 us
    pallas_call x1, Pallas kernels, on_device(): pl.pallas_call(store, name='store', out_shape=tuple((jax.ShapeDtypeStruct...  0.91 us

profile of v5, /device:TPU:128, one launch (start us, length us, event | category | flops | bytes accessed | tf_op | source)
XLA Modules:
  0.0 32.9 jit_solution(4429840478374716245)
XLA Ops:
  0.6 31.3 %layer.1 = (bf16[1,128,1024]{2,1,0:T(8,128)(2,1)S(1)}, f32[1,1,2,128,256]{4,3,2,1,0:T(8,128)S(1)}, f32[1,1,256,128]{3,2,1,0:T(8,128)S(1)}) custom-call(bf16[1,128,1024]{2,1,0:T(8,128)(2,1)} %refs_0_.1, bf16[1,128,1024]{2,1,0:T(8,128)(2,1)} %refs_1_.1, bf16[1,128,1024]{2,1,0:T(8,128)(2,1)} %refs_2_.1, f32[1,1,1024]{2,1,0:T(1,128)} %refs_3_.1, ...), custom_call_target="tpu_custom_call" | custom-call | tf_op jit(solution)/shard_map/layer/pallas_call | solution.py:450
  32.0 0.9 %store.1 = (bf16[1,128,1024]{2,1,0:T(8,128)(2,1)}, f32[1,1,2,128,256]{4,3,2,1,0:T(8,128)}, f32[1,1,256,128]{3,2,1,0:T(8,128)}) custom-call(bf16[1,128,1024]{2,1,0:T(8,128)(2,1)S(1)} %get-tuple-element.6.refs_0_, f32[1,1,2,128,256]{4,3,2,1,0:T(8,128)S(1)} %get-tuple-element.7.refs_1_, f32[1,1,256,128]{3,2,1,0:T(8,128)S(1)} %get-tuple-element.8.refs_2_), custom_call_target="tpu_custom_call" | custom-call | tf_op jit(solution)/shard_map/store/pallas_call | solution.py:519
